TPU v7x, 512 devices: a whole 4x8x8 slice. The times are simulated.
512 devices in a mesh: team: 16 (over y, core), tm: 32 (over x, z).
Axes of the slice: x: 4, y: 8, z: 8, core: 2. Of those that a mesh axis runs over, the one named last changes fastest.
Arguments:
- transitions: float32 [16, 32, 512, 512], P('team', 'tm'), may hold values from -0.25 to 1.25
- states: float32 [16, 32, 64, 512], P('team', 'tm'), may hold values from -1 to 1
- cotangent: float32 [16, 32, 64, 512], P('team', 'tm'), may hold values from -2.4 to 2.4
- terminal: float32 [16, 64, 512], P('team'), may hold values from -6 to 6
- incidence: int32 [16, 32, 32, 2048], P('team', 'tm'), may hold values 0 or 1
- measured: float32 [16, 32, 64, 32], P('team', 'tm'), may hold values from -0.12 to 0.12
- obs_gain: float32 [16, 512], P('team'), may hold values from -6 to 6
Outputs:
- adjoint: float32 [16, 32, 64, 512], P('team', 'tm')
- grad_transitions: bfloat16 [16, 32, 512, 512], P('team', 'tm')
All inputs are finite; a program needn't handle non-finite values. No bound on the sum of `incidence` on one device may be relied on, other than what follows from the above.
Results may differ from a plain program's by a relative error of at most 0.001.
Values sent between devices are 32-bit elements; how exact they have to be, the bound alone decides.
No kernel may reach another device: no remote copies, remote signals or barrier semaphores. Data moves between devices by JAX's collectives and lax.ppermute only.
A program may use at most 64 MiB of HBM per device.

v0:
```python
import jax
import jax.numpy as jnp
from jax import lax
from jax.sharding import PartitionSpec as P

STATES = 16
TEAM_STATES = 512
COLS = 64
HIGHEST = lax.Precision.HIGHEST


def from_behind(block, axis, distance):
    devices = range(lax.axis_size(axis))
    route = [(i - distance, i) for i in devices if i - distance in devices]
    return lax.ppermute(block, axis, route)


def matmul(left, right):
    return jnp.dot(left, right, precision=HIGHEST)


def shards(transitions, states, cotangent, terminal, incidence, measured, obs_gain):
    step_count = transitions.shape[1]
    matrices = transitions[0]
    incident = incidence[0].astype(jnp.float32)
    partial_value = jnp.einsum("scr,srl->scl", measured[0], incident, precision=HIGHEST)
    landmark = lax.psum(partial_value, "team")
    injection = jnp.einsum("scl,srl->scr", landmark, incident, precision=HIGHEST)
    driven = cotangent[0] + jnp.repeat(injection, STATES, axis=2) * obs_gain[0][None, None, :]
    offset = jnp.zeros((COLS, TEAM_STATES), jnp.float32)
    moment = 0
    offset = matmul(offset, matrices[moment]) + driven[moment]
    is_last = lax.axis_index("tm") == lax.axis_size("tm") - 1
    start_cot = jnp.where(is_last, terminal[0], jnp.zeros_like(terminal[0]))

    def advance_steps(turn, carried):
        outgoing = carried
        outgoing = matmul(outgoing, matrices[0])
        outgoing = outgoing + offset
        return from_behind(outgoing, "tm", -1) + start_cot

    incoming = lax.fori_loop(0, lax.axis_size("tm") - 1, advance_steps, start_cot)
    running = incoming
    adjoint_list = [None] * step_count
    grad_list = [None] * step_count
    moment = 0
    grad_now = jnp.einsum("cn,cm->nm", running, states[0, moment], precision=HIGHEST)
    grad_list[moment] = grad_now.astype(jnp.bfloat16)
    running = matmul(running, matrices[moment]) + driven[moment]
    adjoint_list[moment] = running
    adjoint = jnp.stack(adjoint_list)[None]
    grad_transitions = jnp.stack(grad_list)[None]
    return (adjoint, grad_transitions)


def solution(mesh):
    placed = (
        P("team", "tm", None, None),
        P("team", "tm", None, None),
        P("team", "tm", None, None),
        P("team", None, None),
        P("team", "tm", None, None),
        P("team", "tm", None, None),
        P("team", None),
    )
    return jax.shard_map(
        shards,
        mesh=mesh,
        in_specs=placed,
        out_specs=(P("team", "tm", None, None), P("team", "tm", None, None)),
        check_vma=False,
    )
```

profile of v0, /device:TPU:30, one launch (start us, length us, event | category | flops | bytes accessed | tf_op | source)
XLA Modules:
  0.0 454.6 jit_solution(4725242785528667431)
XLA Ops:
  10.6 120.1 %all-reduce.2.cloned.1.call-done = f32[64,2048]{1,0:T(8,128)} async-done(((f32[64,2048]{1,0:T(8,128)}), f32[64,2048]{1,0:T(8,128)}) %all-reduce.2.cloned.1.call-update) | async-done | bytes 524304 | tf_op jit(solution)/shard_map/psum | solution.py:27
  134.0 310.5 %while.10 = (s32[]{:T(128)}, f32[64,512]{1,0:T(8,128)S(1)}, f32[1,1,512,512]{3,2,1,0:T(8,128)S(1)}, f32[64,512]{1,0:T(8,128)S(1)}, f32[64,512]{1,0:T(8,128)S(1)}, /*index=5*/s32[]{:T(128)}) while((s32[]{:T(128)}, f32[64,512]{1,0:T(8,128)S(1)}, f32[1,1,512,512]{3,2,1,0:T(8,128)S(1)}, f32[64,512]{1,0:T(8,128)S(1)}, f32[64,512]{1,0:T(8,128)S(1)}, ...), condition=%wide.region_2.3_spmd, body=%wide.region_1.2_spmd.sunk | while | flops 201392128 | bytes 2359405 | solution.py:42
  145.5 6.5 %collective-permute-start = (f32[64,512]{1,0:T(8,128)S(1)}, f32[64,512]{1,0:T(8,128)S(1)}, u32[]{:S(2)}, u32[]{:S(2)}) collective-permute-start(f32[64,512]{1,0:T(8,128)S(1)} %convolution_add_fusion.4), channel_id=1, source_target_pairs={{1,0},{2,1},{3,2},{4,3},{5,4},{6,5},{7,6},{8,7},{9,8},{10,9},{11,1... | collective-permute-start | bytes 393224 | tf_op jit(solution)/shard_map/while/body/eval_jaxpr/ppermute | solution.py:15
  155.8 6.5 %collective-permute-start = (f32[64,512]{1,0:T(8,128)S(1)}, f32[64,512]{1,0:T(8,128)S(1)}, u32[]{:S(2)}, u32[]{:S(2)}) collective-permute-start(f32[64,512]{1,0:T(8,128)S(1)} %convolution_add_fusion.4), channel_id=1, source_target_pairs={{1,0},{2,1},{3,2},{4,3},{5,4},{6,5},{7,6},{8,7},{9,8},{10,9},{11,1... | collective-permute-start | bytes 393224 | tf_op jit(solution)/shard_map/while/body/eval_jaxpr/ppermute | solution.py:15
  165.6 6.5 %collective-permute-start = (f32[64,512]{1,0:T(8,128)S(1)}, f32[64,512]{1,0:T(8,128)S(1)}, u32[]{:S(2)}, u32[]{:S(2)}) collective-permute-start(f32[64,512]{1,0:T(8,128)S(1)} %convolution_add_fusion.4), channel_id=1, source_target_pairs={{1,0},{2,1},{3,2},{4,3},{5,4},{6,5},{7,6},{8,7},{9,8},{10,9},{11,1... | collective-permute-start | bytes 393224 | tf_op jit(solution)/shard_map/while/body/eval_jaxpr/ppermute | solution.py:15
  175.3 6.5 %collective-permute-start = (f32[64,512]{1,0:T(8,128)S(1)}, f32[64,512]{1,0:T(8,128)S(1)}, u32[]{:S(2)}, u32[]{:S(2)}) collective-permute-start(f32[64,512]{1,0:T(8,128)S(1)} %convolution_add_fusion.4), channel_id=1, source_target_pairs={{1,0},{2,1},{3,2},{4,3},{5,4},{6,5},{7,6},{8,7},{9,8},{10,9},{11,1... | collective-permute-start | bytes 393224 | tf_op jit(solution)/shard_map/while/body/eval_jaxpr/ppermute | solution.py:15
  185.1 6.5 %collective-permute-start = (f32[64,512]{1,0:T(8,128)S(1)}, f32[64,512]{1,0:T(8,128)S(1)}, u32[]{:S(2)}, u32[]{:S(2)}) collective-permute-start(f32[64,512]{1,0:T(8,128)S(1)} %convolution_add_fusion.4), channel_id=1, source_target_pairs={{1,0},{2,1},{3,2},{4,3},{5,4},{6,5},{7,6},{8,7},{9,8},{10,9},{11,1... | collective-permute-start | bytes 393224 | tf_op jit(solution)/shard_map/while/body/eval_jaxpr/ppermute | solution.py:15
  194.8 6.5 %collective-permute-start = (f32[64,512]{1,0:T(8,128)S(1)}, f32[64,512]{1,0:T(8,128)S(1)}, u32[]{:S(2)}, u32[]{:S(2)}) collective-permute-start(f32[64,512]{1,0:T(8,128)S(1)} %convolution_add_fusion.4), channel_id=1, source_target_pairs={{1,0},{2,1},{3,2},{4,3},{5,4},{6,5},{7,6},{8,7},{9,8},{10,9},{11,1... | collective-permute-start | bytes 393224 | tf_op jit(solution)/shard_map/while/body/eval_jaxpr/ppermute | solution.py:15
  214.6 6.5 %collective-permute-start = (f32[64,512]{1,0:T(8,128)S(1)}, f32[64,512]{1,0:T(8,128)S(1)}, u32[]{:S(2)}, u32[]{:S(2)}) collective-permute-start(f32[64,512]{1,0:T(8,128)S(1)} %convolution_add_fusion.4), channel_id=1, source_target_pairs={{1,0},{2,1},{3,2},{4,3},{5,4},{6,5},{7,6},{8,7},{9,8},{10,9},{11,1... | collective-permute-start | bytes 393224 | tf_op jit(solution)/shard_map/while/body/eval_jaxpr/ppermute | solution.py:15
  225.8 6.5 %collective-permute-start = (f32[64,512]{1,0:T(8,128)S(1)}, f32[64,512]{1,0:T(8,128)S(1)}, u32[]{:S(2)}, u32[]{:S(2)}) collective-permute-start(f32[64,512]{1,0:T(8,128)S(1)} %convolution_add_fusion.4), channel_id=1, source_target_pairs={{1,0},{2,1},{3,2},{4,3},{5,4},{6,5},{7,6},{8,7},{9,8},{10,9},{11,1... | collective-permute-start | bytes 393224 | tf_op jit(solution)/shard_map/while/body/eval_jaxpr/ppermute | solution.py:15
  236.0 6.5 %collective-permute-start = (f32[64,512]{1,0:T(8,128)S(1)}, f32[64,512]{1,0:T(8,128)S(1)}, u32[]{:S(2)}, u32[]{:S(2)}) collective-permute-start(f32[64,512]{1,0:T(8,128)S(1)} %convolution_add_fusion.4), channel_id=1, source_target_pairs={{1,0},{2,1},{3,2},{4,3},{5,4},{6,5},{7,6},{8,7},{9,8},{10,9},{11,1... | collective-permute-start | bytes 393224 | tf_op jit(solution)/shard_map/while/body/eval_jaxpr/ppermute | solution.py:15
  255.5 6.5 %collective-permute-start = (f32[64,512]{1,0:T(8,128)S(1)}, f32[64,512]{1,0:T(8,128)S(1)}, u32[]{:S(2)}, u32[]{:S(2)}) collective-permute-start(f32[64,512]{1,0:T(8,128)S(1)} %convolution_add_fusion.4), channel_id=1, source_target_pairs={{1,0},{2,1},{3,2},{4,3},{5,4},{6,5},{7,6},{8,7},{9,8},{10,9},{11,1... | collective-permute-start | bytes 393224 | tf_op jit(solution)/shard_map/while/body/eval_jaxpr/ppermute | solution.py:15
  265.3 6.5 %collective-permute-start = (f32[64,512]{1,0:T(8,128)S(1)}, f32[64,512]{1,0:T(8,128)S(1)}, u32[]{:S(2)}, u32[]{:S(2)}) collective-permute-start(f32[64,512]{1,0:T(8,128)S(1)} %convolution_add_fusion.4), channel_id=1, source_target_pairs={{1,0},{2,1},{3,2},{4,3},{5,4},{6,5},{7,6},{8,7},{9,8},{10,9},{11,1... | collective-permute-start | bytes 393224 | tf_op jit(solution)/shard_map/while/body/eval_jaxpr/ppermute | solution.py:15
  294.8 6.5 %collective-permute-start = (f32[64,512]{1,0:T(8,128)S(1)}, f32[64,512]{1,0:T(8,128)S(1)}, u32[]{:S(2)}, u32[]{:S(2)}) collective-permute-start(f32[64,512]{1,0:T(8,128)S(1)} %convolution_add_fusion.4), channel_id=1, source_target_pairs={{1,0},{2,1},{3,2},{4,3},{5,4},{6,5},{7,6},{8,7},{9,8},{10,9},{11,1... | collective-permute-start | bytes 393224 | tf_op jit(solution)/shard_map/while/body/eval_jaxpr/ppermute | solution.py:15
  306.0 6.5 %collective-permute-start = (f32[64,512]{1,0:T(8,128)S(1)}, f32[64,512]{1,0:T(8,128)S(1)}, u32[]{:S(2)}, u32[]{:S(2)}) collective-permute-start(f32[64,512]{1,0:T(8,128)S(1)} %convolution_add_fusion.4), channel_id=1, source_target_pairs={{1,0},{2,1},{3,2},{4,3},{5,4},{6,5},{7,6},{8,7},{9,8},{10,9},{11,1... | collective-permute-start | bytes 393224 | tf_op jit(solution)/shard_map/while/body/eval_jaxpr/ppermute | solution.py:15
  316.2 6.5 %collective-permute-start = (f32[64,512]{1,0:T(8,128)S(1)}, f32[64,512]{1,0:T(8,128)S(1)}, u32[]{:S(2)}, u32[]{:S(2)}) collective-permute-start(f32[64,512]{1,0:T(8,128)S(1)} %convolution_add_fusion.4), channel_id=1, source_target_pairs={{1,0},{2,1},{3,2},{4,3},{5,4},{6,5},{7,6},{8,7},{9,8},{10,9},{11,1... | collective-permute-start | bytes 393224 | tf_op jit(solution)/shard_map/while/body/eval_jaxpr/ppermute | solution.py:15
  326.0 6.5 %collective-permute-start = (f32[64,512]{1,0:T(8,128)S(1)}, f32[64,512]{1,0:T(8,128)S(1)}, u32[]{:S(2)}, u32[]{:S(2)}) collective-permute-start(f32[64,512]{1,0:T(8,128)S(1)} %convolution_add_fusion.4), channel_id=1, source_target_pairs={{1,0},{2,1},{3,2},{4,3},{5,4},{6,5},{7,6},{8,7},{9,8},{10,9},{11,1... | collective-permute-start | bytes 393224 | tf_op jit(solution)/shard_map/while/body/eval_jaxpr/ppermute | solution.py:15
  355.3 6.5 %collective-permute-start = (f32[64,512]{1,0:T(8,128)S(1)}, f32[64,512]{1,0:T(8,128)S(1)}, u32[]{:S(2)}, u32[]{:S(2)}) collective-permute-start(f32[64,512]{1,0:T(8,128)S(1)} %convolution_add_fusion.4), channel_id=1, source_target_pairs={{1,0},{2,1},{3,2},{4,3},{5,4},{6,5},{7,6},{8,7},{9,8},{10,9},{11,1... | collective-permute-start | bytes 393224 | tf_op jit(solution)/shard_map/while/body/eval_jaxpr/ppermute | solution.py:15
  365.0 6.5 %collective-permute-start = (f32[64,512]{1,0:T(8,128)S(1)}, f32[64,512]{1,0:T(8,128)S(1)}, u32[]{:S(2)}, u32[]{:S(2)}) collective-permute-start(f32[64,512]{1,0:T(8,128)S(1)} %convolution_add_fusion.4), channel_id=1, source_target_pairs={{1,0},{2,1},{3,2},{4,3},{5,4},{6,5},{7,6},{8,7},{9,8},{10,9},{11,1... | collective-permute-start | bytes 393224 | tf_op jit(solution)/shard_map/while/body/eval_jaxpr/ppermute | solution.py:15
  375.1 6.5 %collective-permute-start = (f32[64,512]{1,0:T(8,128)S(1)}, f32[64,512]{1,0:T(8,128)S(1)}, u32[]{:S(2)}, u32[]{:S(2)}) collective-permute-start(f32[64,512]{1,0:T(8,128)S(1)} %convolution_add_fusion.4), channel_id=1, source_target_pairs={{1,0},{2,1},{3,2},{4,3},{5,4},{6,5},{7,6},{8,7},{9,8},{10,9},{11,1... | collective-permute-start | bytes 393224 | tf_op jit(solution)/shard_map/while/body/eval_jaxpr/ppermute | solution.py:15
  386.2 6.5 %collective-permute-start = (f32[64,512]{1,0:T(8,128)S(1)}, f32[64,512]{1,0:T(8,128)S(1)}, u32[]{:S(2)}, u32[]{:S(2)}) collective-permute-start(f32[64,512]{1,0:T(8,128)S(1)} %convolution_add_fusion.4), channel_id=1, source_target_pairs={{1,0},{2,1},{3,2},{4,3},{5,4},{6,5},{7,6},{8,7},{9,8},{10,9},{11,1... | collective-permute-start | bytes 393224 | tf_op jit(solution)/shard_map/while/body/eval_jaxpr/ppermute | solution.py:15
  396.4 6.5 %collective-permute-start = (f32[64,512]{1,0:T(8,128)S(1)}, f32[64,512]{1,0:T(8,128)S(1)}, u32[]{:S(2)}, u32[]{:S(2)}) collective-permute-start(f32[64,512]{1,0:T(8,128)S(1)} %convolution_add_fusion.4), channel_id=1, source_target_pairs={{1,0},{2,1},{3,2},{4,3},{5,4},{6,5},{7,6},{8,7},{9,8},{10,9},{11,1... | collective-permute-start | bytes 393224 | tf_op jit(solution)/shard_map/while/body/eval_jaxpr/ppermute | solution.py:15
  416.0 6.5 %collective-permute-start = (f32[64,512]{1,0:T(8,128)S(1)}, f32[64,512]{1,0:T(8,128)S(1)}, u32[]{:S(2)}, u32[]{:S(2)}) collective-permute-start(f32[64,512]{1,0:T(8,128)S(1)} %convolution_add_fusion.4), channel_id=1, source_target_pairs={{1,0},{2,1},{3,2},{4,3},{5,4},{6,5},{7,6},{8,7},{9,8},{10,9},{11,1... | collective-permute-start | bytes 393224 | tf_op jit(solution)/shard_map/while/body/eval_jaxpr/ppermute | solution.py:15
  425.8 6.5 %collective-permute-start = (f32[64,512]{1,0:T(8,128)S(1)}, f32[64,512]{1,0:T(8,128)S(1)}, u32[]{:S(2)}, u32[]{:S(2)}) collective-permute-start(f32[64,512]{1,0:T(8,128)S(1)} %convolution_add_fusion.4), channel_id=1, source_target_pairs={{1,0},{2,1},{3,2},{4,3},{5,4},{6,5},{7,6},{8,7},{9,8},{10,9},{11,1... | collective-permute-start | bytes 393224 | tf_op jit(solution)/shard_map/while/body/eval_jaxpr/ppermute | solution.py:15
  (125 shorter events, 177.1 us)
Async XLA Ops:
  7.2 123.5 %all-reduce.2.cloned.1.call-start = ((), (), s32[]{:S(2)}) async-start(), calls=%async_computation | async-start | bytes 1048576 | tf_op jit(solution)/shard_map/psum | solution.py:27
  134.8 10.0 %collective-permute-start = (f32[64,512]{1,0:T(8,128)S(1)}, f32[64,512]{1,0:T(8,128)S(1)}, u32[]{:S(2)}, u32[]{:S(2)}) collective-permute-start(f32[64,512]{1,0:T(8,128)S(1)} %convolution_add_fusion.4), channel_id=1, source_target_pairs={{1,0},{2,1},{3,2},{4,3},{5,4},{6,5},{7,6},{8,7},{9,8},{10,9},{11,1... | collective-permute-start | bytes 393224 | tf_op jit(solution)/shard_map/while/body/eval_jaxpr/ppermute | solution.py:15
  145.5 9.4 %collective-permute-start = (f32[64,512]{1,0:T(8,128)S(1)}, f32[64,512]{1,0:T(8,128)S(1)}, u32[]{:S(2)}, u32[]{:S(2)}) collective-permute-start(f32[64,512]{1,0:T(8,128)S(1)} %convolution_add_fusion.4), channel_id=1, source_target_pairs={{1,0},{2,1},{3,2},{4,3},{5,4},{6,5},{7,6},{8,7},{9,8},{10,9},{11,1... | collective-permute-start | bytes 393224 | tf_op jit(solution)/shard_map/while/body/eval_jaxpr/ppermute | solution.py:15
  155.8 9.0 %collective-permute-start = (f32[64,512]{1,0:T(8,128)S(1)}, f32[64,512]{1,0:T(8,128)S(1)}, u32[]{:S(2)}, u32[]{:S(2)}) collective-permute-start(f32[64,512]{1,0:T(8,128)S(1)} %convolution_add_fusion.4), channel_id=1, source_target_pairs={{1,0},{2,1},{3,2},{4,3},{5,4},{6,5},{7,6},{8,7},{9,8},{10,9},{11,1... | collective-permute-start | bytes 393224 | tf_op jit(solution)/shard_map/while/body/eval_jaxpr/ppermute | solution.py:15
  175.3 9.0 %collective-permute-start = (f32[64,512]{1,0:T(8,128)S(1)}, f32[64,512]{1,0:T(8,128)S(1)}, u32[]{:S(2)}, u32[]{:S(2)}) collective-permute-start(f32[64,512]{1,0:T(8,128)S(1)} %convolution_add_fusion.4), channel_id=1, source_target_pairs={{1,0},{2,1},{3,2},{4,3},{5,4},{6,5},{7,6},{8,7},{9,8},{10,9},{11,1... | collective-permute-start | bytes 393224 | tf_op jit(solution)/shard_map/while/body/eval_jaxpr/ppermute | solution.py:15
  185.1 9.0 %collective-permute-start = (f32[64,512]{1,0:T(8,128)S(1)}, f32[64,512]{1,0:T(8,128)S(1)}, u32[]{:S(2)}, u32[]{:S(2)}) collective-permute-start(f32[64,512]{1,0:T(8,128)S(1)} %convolution_add_fusion.4), channel_id=1, source_target_pairs={{1,0},{2,1},{3,2},{4,3},{5,4},{6,5},{7,6},{8,7},{9,8},{10,9},{11,1... | collective-permute-start | bytes 393224 | tf_op jit(solution)/shard_map/while/body/eval_jaxpr/ppermute | solution.py:15
  204.6 9.2 %collective-permute-start = (f32[64,512]{1,0:T(8,128)S(1)}, f32[64,512]{1,0:T(8,128)S(1)}, u32[]{:S(2)}, u32[]{:S(2)}) collective-permute-start(f32[64,512]{1,0:T(8,128)S(1)} %convolution_add_fusion.4), channel_id=1, source_target_pairs={{1,0},{2,1},{3,2},{4,3},{5,4},{6,5},{7,6},{8,7},{9,8},{10,9},{11,1... | collective-permute-start | bytes 393224 | tf_op jit(solution)/shard_map/while/body/eval_jaxpr/ppermute | solution.py:15
  214.6 10.4 %collective-permute-start = (f32[64,512]{1,0:T(8,128)S(1)}, f32[64,512]{1,0:T(8,128)S(1)}, u32[]{:S(2)}, u32[]{:S(2)}) collective-permute-start(f32[64,512]{1,0:T(8,128)S(1)} %convolution_add_fusion.4), channel_id=1, source_target_pairs={{1,0},{2,1},{3,2},{4,3},{5,4},{6,5},{7,6},{8,7},{9,8},{10,9},{11,1... | collective-permute-start | bytes 393224 | tf_op jit(solution)/shard_map/while/body/eval_jaxpr/ppermute | solution.py:15
  225.8 9.4 %collective-permute-start = (f32[64,512]{1,0:T(8,128)S(1)}, f32[64,512]{1,0:T(8,128)S(1)}, u32[]{:S(2)}, u32[]{:S(2)}) collective-permute-start(f32[64,512]{1,0:T(8,128)S(1)} %convolution_add_fusion.4), channel_id=1, source_target_pairs={{1,0},{2,1},{3,2},{4,3},{5,4},{6,5},{7,6},{8,7},{9,8},{10,9},{11,1... | collective-permute-start | bytes 393224 | tf_op jit(solution)/shard_map/while/body/eval_jaxpr/ppermute | solution.py:15
  236.0 9.0 %collective-permute-start = (f32[64,512]{1,0:T(8,128)S(1)}, f32[64,512]{1,0:T(8,128)S(1)}, u32[]{:S(2)}, u32[]{:S(2)}) collective-permute-start(f32[64,512]{1,0:T(8,128)S(1)} %convolution_add_fusion.4), channel_id=1, source_target_pairs={{1,0},{2,1},{3,2},{4,3},{5,4},{6,5},{7,6},{8,7},{9,8},{10,9},{11,1... | collective-permute-start | bytes 393224 | tf_op jit(solution)/shard_map/while/body/eval_jaxpr/ppermute | solution.py:15
  255.5 9.0 %collective-permute-start = (f32[64,512]{1,0:T(8,128)S(1)}, f32[64,512]{1,0:T(8,128)S(1)}, u32[]{:S(2)}, u32[]{:S(2)}) collective-permute-start(f32[64,512]{1,0:T(8,128)S(1)} %convolution_add_fusion.4), channel_id=1, source_target_pairs={{1,0},{2,1},{3,2},{4,3},{5,4},{6,5},{7,6},{8,7},{9,8},{10,9},{11,1... | collective-permute-start | bytes 393224 | tf_op jit(solution)/shard_map/while/body/eval_jaxpr/ppermute | solution.py:15
  265.3 9.0 %collective-permute-start = (f32[64,512]{1,0:T(8,128)S(1)}, f32[64,512]{1,0:T(8,128)S(1)}, u32[]{:S(2)}, u32[]{:S(2)}) collective-permute-start(f32[64,512]{1,0:T(8,128)S(1)} %convolution_add_fusion.4), channel_id=1, source_target_pairs={{1,0},{2,1},{3,2},{4,3},{5,4},{6,5},{7,6},{8,7},{9,8},{10,9},{11,1... | collective-permute-start | bytes 393224 | tf_op jit(solution)/shard_map/while/body/eval_jaxpr/ppermute | solution.py:15
  284.8 9.2 %collective-permute-start = (f32[64,512]{1,0:T(8,128)S(1)}, f32[64,512]{1,0:T(8,128)S(1)}, u32[]{:S(2)}, u32[]{:S(2)}) collective-permute-start(f32[64,512]{1,0:T(8,128)S(1)} %convolution_add_fusion.4), channel_id=1, source_target_pairs={{1,0},{2,1},{3,2},{4,3},{5,4},{6,5},{7,6},{8,7},{9,8},{10,9},{11,1... | collective-permute-start | bytes 393224 | tf_op jit(solution)/shard_map/while/body/eval_jaxpr/ppermute | solution.py:15
  294.8 10.3 %collective-permute-start = (f32[64,512]{1,0:T(8,128)S(1)}, f32[64,512]{1,0:T(8,128)S(1)}, u32[]{:S(2)}, u32[]{:S(2)}) collective-permute-start(f32[64,512]{1,0:T(8,128)S(1)} %convolution_add_fusion.4), channel_id=1, source_target_pairs={{1,0},{2,1},{3,2},{4,3},{5,4},{6,5},{7,6},{8,7},{9,8},{10,9},{11,1... | collective-permute-start | bytes 393224 | tf_op jit(solution)/shard_map/while/body/eval_jaxpr/ppermute | solution.py:15
  306.0 9.5 %collective-permute-start = (f32[64,512]{1,0:T(8,128)S(1)}, f32[64,512]{1,0:T(8,128)S(1)}, u32[]{:S(2)}, u32[]{:S(2)}) collective-permute-start(f32[64,512]{1,0:T(8,128)S(1)} %convolution_add_fusion.4), channel_id=1, source_target_pairs={{1,0},{2,1},{3,2},{4,3},{5,4},{6,5},{7,6},{8,7},{9,8},{10,9},{11,1... | collective-permute-start | bytes 393224 | tf_op jit(solution)/shard_map/while/body/eval_jaxpr/ppermute | solution.py:15
  316.2 9.0 %collective-permute-start = (f32[64,512]{1,0:T(8,128)S(1)}, f32[64,512]{1,0:T(8,128)S(1)}, u32[]{:S(2)}, u32[]{:S(2)}) collective-permute-start(f32[64,512]{1,0:T(8,128)S(1)} %convolution_add_fusion.4), channel_id=1, source_target_pairs={{1,0},{2,1},{3,2},{4,3},{5,4},{6,5},{7,6},{8,7},{9,8},{10,9},{11,1... | collective-permute-start | bytes 393224 | tf_op jit(solution)/shard_map/while/body/eval_jaxpr/ppermute | solution.py:15
  326.0 9.0 %collective-permute-start = (f32[64,512]{1,0:T(8,128)S(1)}, f32[64,512]{1,0:T(8,128)S(1)}, u32[]{:S(2)}, u32[]{:S(2)}) collective-permute-start(f32[64,512]{1,0:T(8,128)S(1)} %convolution_add_fusion.4), channel_id=1, source_target_pairs={{1,0},{2,1},{3,2},{4,3},{5,4},{6,5},{7,6},{8,7},{9,8},{10,9},{11,1... | collective-permute-start | bytes 393224 | tf_op jit(solution)/shard_map/while/body/eval_jaxpr/ppermute | solution.py:15
  355.3 9.0 %collective-permute-start = (f32[64,512]{1,0:T(8,128)S(1)}, f32[64,512]{1,0:T(8,128)S(1)}, u32[]{:S(2)}, u32[]{:S(2)}) collective-permute-start(f32[64,512]{1,0:T(8,128)S(1)} %convolution_add_fusion.4), channel_id=1, source_target_pairs={{1,0},{2,1},{3,2},{4,3},{5,4},{6,5},{7,6},{8,7},{9,8},{10,9},{11,1... | collective-permute-start | bytes 393224 | tf_op jit(solution)/shard_map/while/body/eval_jaxpr/ppermute | solution.py:15
  365.0 9.2 %collective-permute-start = (f32[64,512]{1,0:T(8,128)S(1)}, f32[64,512]{1,0:T(8,128)S(1)}, u32[]{:S(2)}, u32[]{:S(2)}) collective-permute-start(f32[64,512]{1,0:T(8,128)S(1)} %convolution_add_fusion.4), channel_id=1, source_target_pairs={{1,0},{2,1},{3,2},{4,3},{5,4},{6,5},{7,6},{8,7},{9,8},{10,9},{11,1... | collective-permute-start | bytes 393224 | tf_op jit(solution)/shard_map/while/body/eval_jaxpr/ppermute | solution.py:15
  375.1 10.4 %collective-permute-start = (f32[64,512]{1,0:T(8,128)S(1)}, f32[64,512]{1,0:T(8,128)S(1)}, u32[]{:S(2)}, u32[]{:S(2)}) collective-permute-start(f32[64,512]{1,0:T(8,128)S(1)} %convolution_add_fusion.4), channel_id=1, source_target_pairs={{1,0},{2,1},{3,2},{4,3},{5,4},{6,5},{7,6},{8,7},{9,8},{10,9},{11,1... | collective-permute-start | bytes 393224 | tf_op jit(solution)/shard_map/while/body/eval_jaxpr/ppermute | solution.py:15
  386.2 9.4 %collective-permute-start = (f32[64,512]{1,0:T(8,128)S(1)}, f32[64,512]{1,0:T(8,128)S(1)}, u32[]{:S(2)}, u32[]{:S(2)}) collective-permute-start(f32[64,512]{1,0:T(8,128)S(1)} %convolution_add_fusion.4), channel_id=1, source_target_pairs={{1,0},{2,1},{3,2},{4,3},{5,4},{6,5},{7,6},{8,7},{9,8},{10,9},{11,1... | collective-permute-start | bytes 393224 | tf_op jit(solution)/shard_map/while/body/eval_jaxpr/ppermute | solution.py:15
  396.4 9.0 %collective-permute-start = (f32[64,512]{1,0:T(8,128)S(1)}, f32[64,512]{1,0:T(8,128)S(1)}, u32[]{:S(2)}, u32[]{:S(2)}) collective-permute-start(f32[64,512]{1,0:T(8,128)S(1)} %convolution_add_fusion.4), channel_id=1, source_target_pairs={{1,0},{2,1},{3,2},{4,3},{5,4},{6,5},{7,6},{8,7},{9,8},{10,9},{11,1... | collective-permute-start | bytes 393224 | tf_op jit(solution)/shard_map/while/body/eval_jaxpr/ppermute | solution.py:15
  416.0 9.0 %collective-permute-start = (f32[64,512]{1,0:T(8,128)S(1)}, f32[64,512]{1,0:T(8,128)S(1)}, u32[]{:S(2)}, u32[]{:S(2)}) collective-permute-start(f32[64,512]{1,0:T(8,128)S(1)} %convolution_add_fusion.4), channel_id=1, source_target_pairs={{1,0},{2,1},{3,2},{4,3},{5,4},{6,5},{7,6},{8,7},{9,8},{10,9},{11,1... | collective-permute-start | bytes 393224 | tf_op jit(solution)/shard_map/while/body/eval_jaxpr/ppermute | solution.py:15
  425.8 9.0 %collective-permute-start = (f32[64,512]{1,0:T(8,128)S(1)}, f32[64,512]{1,0:T(8,128)S(1)}, u32[]{:S(2)}, u32[]{:S(2)}) collective-permute-start(f32[64,512]{1,0:T(8,128)S(1)} %convolution_add_fusion.4), channel_id=1, source_target_pairs={{1,0},{2,1},{3,2},{4,3},{5,4},{6,5},{7,6},{8,7},{9,8},{10,9},{11,1... | collective-permute-start | bytes 393224 | tf_op jit(solution)/shard_map/while/body/eval_jaxpr/ppermute | solution.py:15
  (14 other events, 757.1 us)
Sparse Core Ops, SparseCore 0:
  10.9 119.8 all-reduce.1
where the time goes:
time: 456 us; the launch traced here: 455 us
  waiting for transfers between devices  206 us (45%)
  starting transfers between devices  200 us (44%)
  matrix products  31.3 us (7%)
  between operations  14.1 us (3%)
    ppermute x31, starting transfers between devices, from_behind(): return lax.ppermute(block, axis, route)  200 us
    psum x1, waiting for transfers between devices, shards(): landmark = lax.psum(partial_value, 'team')  120 us
    ppermute x31, waiting for transfers between devices, from_behind(): return lax.ppermute(block, axis, route)  85.5 us
    dot_general x33, matrix products, matmul(): return jnp.dot(left, right, precision=HIGHEST)  25.5 us
  transfers between devices with their start and end apart: 32, of which 32 were waited for; matrix products, arithmetic and copies ran while one was open for 0% of the time, Pallas kernels for 0%

commit v1 on v0

--- a/solution.py
+++ b/solution.py
@@ -24,7 +24,7 @@
     matrices = transitions[0]
     incident = incidence[0].astype(jnp.float32)
     partial_value = jnp.einsum("scr,srl->scl", measured[0], incident, precision=HIGHEST)
-    landmark = lax.psum(partial_value, "team")
+    landmark = jnp.sum(lax.all_gather(partial_value, "team"), axis=0)
     injection = jnp.einsum("scl,srl->scr", landmark, incident, precision=HIGHEST)
     driven = cotangent[0] + jnp.repeat(injection, STATES, axis=2) * obs_gain[0][None, None, :]
     offset = jnp.zeros((COLS, TEAM_STATES), jnp.float32)

time: 456 us -> 399 us (0.88)
  waiting for transfers between devices: 206 us -> 147 us
    psum x1 -> x0, waiting for transfers between devices: 120 us -> none  [shards(): landmark = lax.psum(partial_value, 'team')]
    all_gather x0 -> x1, waiting for transfers between devices: none -> 63.2 us  [shards(): landmark = jnp.sum(lax.all_gather(partial_value, 'team'), axis=0)]
where the time goes in v1:
time: 399 us; the launch traced here: 398 us
  starting transfers between devices  200 us (50%)
  waiting for transfers between devices  147 us (37%)
  matrix products  30.4 us (8%)
  between operations  14.2 us (4%)
  other arithmetic  4.55 us (1%)
    ppermute x31, starting transfers between devices, from_behind(): return lax.ppermute(block, axis, route)  200 us
    ppermute x31, waiting for transfers between devices, from_behind(): return lax.ppermute(block, axis, route)  84.1 us
    all_gather x1, waiting for transfers between devices, shards(): landmark = jnp.sum(lax.all_gather(partial_value, 'team'), axis=0)  63.2 us
    dot_general x33, matrix products, matmul(): return jnp.dot(left, right, precision=HIGHEST)  25.5 us
  transfers between devices with their start and end apart: 32, of which 32 were waited for; matrix products, arithmetic and copies ran while one was open for 0% of the time, Pallas kernels for 0%

profile of v1, /device:TPU:30, one launch (start us, length us, event | category | flops | bytes accessed | tf_op | source)
XLA Modules:
  0.0 397.7 jit_solution(16090007423280004034)
XLA Ops:
  9.8 63.2 %all-gather.3.cloned.1.call-done = f32[1024,2048]{1,0:T(8,128)} async-done(((f32[64,2048]{1,0:T(8,128)}), f32[1024,2048]{1,0:T(8,128)}) %all-gather.3.cloned.1.call-update) | async-done | bytes 8388624 | tf_op jit(solution)/shard_map/all_gather | solution.py:27
  78.4 309.2 %while.10 = (s32[]{:T(128)}, f32[64,512]{1,0:T(8,128)S(1)}, f32[1,1,512,512]{3,2,1,0:T(8,128)S(1)}, f32[64,512]{1,0:T(8,128)S(1)}, f32[64,512]{1,0:T(8,128)S(1)}, /*index=5*/s32[]{:T(128)}) while((s32[]{:T(128)}, f32[64,512]{1,0:T(8,128)S(1)}, f32[1,1,512,512]{3,2,1,0:T(8,128)S(1)}, f32[64,512]{1,0:T(8,128)S(1)}, f32[64,512]{1,0:T(8,128)S(1)}, ...), condition=%wide.region_2.3_spmd, body=%wide.region_1.2_spmd.sunk | while | flops 201392128 | bytes 2359405 | solution.py:42
  89.3 6.5 %collective-permute-start = (f32[64,512]{1,0:T(8,128)S(1)}, f32[64,512]{1,0:T(8,128)S(1)}, u32[]{:S(2)}, u32[]{:S(2)}) collective-permute-start(f32[64,512]{1,0:T(8,128)S(1)} %convolution_add_fusion.4), channel_id=1, source_target_pairs={{1,0},{2,1},{3,2},{4,3},{5,4},{6,5},{7,6},{8,7},{9,8},{10,9},{11,1... | collective-permute-start | bytes 393224 | tf_op jit(solution)/shard_map/while/body/eval_jaxpr/ppermute | solution.py:15
  99.1 6.5 %collective-permute-start = (f32[64,512]{1,0:T(8,128)S(1)}, f32[64,512]{1,0:T(8,128)S(1)}, u32[]{:S(2)}, u32[]{:S(2)}) collective-permute-start(f32[64,512]{1,0:T(8,128)S(1)} %convolution_add_fusion.4), channel_id=1, source_target_pairs={{1,0},{2,1},{3,2},{4,3},{5,4},{6,5},{7,6},{8,7},{9,8},{10,9},{11,1... | collective-permute-start | bytes 393224 | tf_op jit(solution)/shard_map/while/body/eval_jaxpr/ppermute | solution.py:15
  118.6 6.5 %collective-permute-start = (f32[64,512]{1,0:T(8,128)S(1)}, f32[64,512]{1,0:T(8,128)S(1)}, u32[]{:S(2)}, u32[]{:S(2)}) collective-permute-start(f32[64,512]{1,0:T(8,128)S(1)} %convolution_add_fusion.4), channel_id=1, source_target_pairs={{1,0},{2,1},{3,2},{4,3},{5,4},{6,5},{7,6},{8,7},{9,8},{10,9},{11,1... | collective-permute-start | bytes 393224 | tf_op jit(solution)/shard_map/while/body/eval_jaxpr/ppermute | solution.py:15
  128.3 6.5 %collective-permute-start = (f32[64,512]{1,0:T(8,128)S(1)}, f32[64,512]{1,0:T(8,128)S(1)}, u32[]{:S(2)}, u32[]{:S(2)}) collective-permute-start(f32[64,512]{1,0:T(8,128)S(1)} %convolution_add_fusion.4), channel_id=1, source_target_pairs={{1,0},{2,1},{3,2},{4,3},{5,4},{6,5},{7,6},{8,7},{9,8},{10,9},{11,1... | collective-permute-start | bytes 393224 | tf_op jit(solution)/shard_map/while/body/eval_jaxpr/ppermute | solution.py:15
  148.0 6.5 %collective-permute-start = (f32[64,512]{1,0:T(8,128)S(1)}, f32[64,512]{1,0:T(8,128)S(1)}, u32[]{:S(2)}, u32[]{:S(2)}) collective-permute-start(f32[64,512]{1,0:T(8,128)S(1)} %convolution_add_fusion.4), channel_id=1, source_target_pairs={{1,0},{2,1},{3,2},{4,3},{5,4},{6,5},{7,6},{8,7},{9,8},{10,9},{11,1... | collective-permute-start | bytes 393224 | tf_op jit(solution)/shard_map/while/body/eval_jaxpr/ppermute | solution.py:15
  159.0 6.5 %collective-permute-start = (f32[64,512]{1,0:T(8,128)S(1)}, f32[64,512]{1,0:T(8,128)S(1)}, u32[]{:S(2)}, u32[]{:S(2)}) collective-permute-start(f32[64,512]{1,0:T(8,128)S(1)} %convolution_add_fusion.4), channel_id=1, source_target_pairs={{1,0},{2,1},{3,2},{4,3},{5,4},{6,5},{7,6},{8,7},{9,8},{10,9},{11,1... | collective-permute-start | bytes 393224 | tf_op jit(solution)/shard_map/while/body/eval_jaxpr/ppermute | solution.py:15
  169.3 6.5 %collective-permute-start = (f32[64,512]{1,0:T(8,128)S(1)}, f32[64,512]{1,0:T(8,128)S(1)}, u32[]{:S(2)}, u32[]{:S(2)}) collective-permute-start(f32[64,512]{1,0:T(8,128)S(1)} %convolution_add_fusion.4), channel_id=1, source_target_pairs={{1,0},{2,1},{3,2},{4,3},{5,4},{6,5},{7,6},{8,7},{9,8},{10,9},{11,1... | collective-permute-start | bytes 393224 | tf_op jit(solution)/shard_map/while/body/eval_jaxpr/ppermute | solution.py:15
  179.1 6.5 %collective-permute-start = (f32[64,512]{1,0:T(8,128)S(1)}, f32[64,512]{1,0:T(8,128)S(1)}, u32[]{:S(2)}, u32[]{:S(2)}) collective-permute-start(f32[64,512]{1,0:T(8,128)S(1)} %convolution_add_fusion.4), channel_id=1, source_target_pairs={{1,0},{2,1},{3,2},{4,3},{5,4},{6,5},{7,6},{8,7},{9,8},{10,9},{11,1... | collective-permute-start | bytes 393224 | tf_op jit(solution)/shard_map/while/body/eval_jaxpr/ppermute | solution.py:15
  198.6 6.5 %collective-permute-start = (f32[64,512]{1,0:T(8,128)S(1)}, f32[64,512]{1,0:T(8,128)S(1)}, u32[]{:S(2)}, u32[]{:S(2)}) collective-permute-start(f32[64,512]{1,0:T(8,128)S(1)} %convolution_add_fusion.4), channel_id=1, source_target_pairs={{1,0},{2,1},{3,2},{4,3},{5,4},{6,5},{7,6},{8,7},{9,8},{10,9},{11,1... | collective-permute-start | bytes 393224 | tf_op jit(solution)/shard_map/while/body/eval_jaxpr/ppermute | solution.py:15
  208.4 6.5 %collective-permute-start = (f32[64,512]{1,0:T(8,128)S(1)}, f32[64,512]{1,0:T(8,128)S(1)}, u32[]{:S(2)}, u32[]{:S(2)}) collective-permute-start(f32[64,512]{1,0:T(8,128)S(1)} %convolution_add_fusion.4), channel_id=1, source_target_pairs={{1,0},{2,1},{3,2},{4,3},{5,4},{6,5},{7,6},{8,7},{9,8},{10,9},{11,1... | collective-permute-start | bytes 393224 | tf_op jit(solution)/shard_map/while/body/eval_jaxpr/ppermute | solution.py:15
  228.1 6.5 %collective-permute-start = (f32[64,512]{1,0:T(8,128)S(1)}, f32[64,512]{1,0:T(8,128)S(1)}, u32[]{:S(2)}, u32[]{:S(2)}) collective-permute-start(f32[64,512]{1,0:T(8,128)S(1)} %convolution_add_fusion.4), channel_id=1, source_target_pairs={{1,0},{2,1},{3,2},{4,3},{5,4},{6,5},{7,6},{8,7},{9,8},{10,9},{11,1... | collective-permute-start | bytes 393224 | tf_op jit(solution)/shard_map/while/body/eval_jaxpr/ppermute | solution.py:15
  239.3 6.5 %collective-permute-start = (f32[64,512]{1,0:T(8,128)S(1)}, f32[64,512]{1,0:T(8,128)S(1)}, u32[]{:S(2)}, u32[]{:S(2)}) collective-permute-start(f32[64,512]{1,0:T(8,128)S(1)} %convolution_add_fusion.4), channel_id=1, source_target_pairs={{1,0},{2,1},{3,2},{4,3},{5,4},{6,5},{7,6},{8,7},{9,8},{10,9},{11,1... | collective-permute-start | bytes 393224 | tf_op jit(solution)/shard_map/while/body/eval_jaxpr/ppermute | solution.py:15
  249.6 6.5 %collective-permute-start = (f32[64,512]{1,0:T(8,128)S(1)}, f32[64,512]{1,0:T(8,128)S(1)}, u32[]{:S(2)}, u32[]{:S(2)}) collective-permute-start(f32[64,512]{1,0:T(8,128)S(1)} %convolution_add_fusion.4), channel_id=1, source_target_pairs={{1,0},{2,1},{3,2},{4,3},{5,4},{6,5},{7,6},{8,7},{9,8},{10,9},{11,1... | collective-permute-start | bytes 393224 | tf_op jit(solution)/shard_map/while/body/eval_jaxpr/ppermute | solution.py:15
  259.4 6.5 %collective-permute-start = (f32[64,512]{1,0:T(8,128)S(1)}, f32[64,512]{1,0:T(8,128)S(1)}, u32[]{:S(2)}, u32[]{:S(2)}) collective-permute-start(f32[64,512]{1,0:T(8,128)S(1)} %convolution_add_fusion.4), channel_id=1, source_target_pairs={{1,0},{2,1},{3,2},{4,3},{5,4},{6,5},{7,6},{8,7},{9,8},{10,9},{11,1... | collective-permute-start | bytes 393224 | tf_op jit(solution)/shard_map/while/body/eval_jaxpr/ppermute | solution.py:15
  278.9 6.5 %collective-permute-start = (f32[64,512]{1,0:T(8,128)S(1)}, f32[64,512]{1,0:T(8,128)S(1)}, u32[]{:S(2)}, u32[]{:S(2)}) collective-permute-start(f32[64,512]{1,0:T(8,128)S(1)} %convolution_add_fusion.4), channel_id=1, source_target_pairs={{1,0},{2,1},{3,2},{4,3},{5,4},{6,5},{7,6},{8,7},{9,8},{10,9},{11,1... | collective-permute-start | bytes 393224 | tf_op jit(solution)/shard_map/while/body/eval_jaxpr/ppermute | solution.py:15
  288.6 6.5 %collective-permute-start = (f32[64,512]{1,0:T(8,128)S(1)}, f32[64,512]{1,0:T(8,128)S(1)}, u32[]{:S(2)}, u32[]{:S(2)}) collective-permute-start(f32[64,512]{1,0:T(8,128)S(1)} %convolution_add_fusion.4), channel_id=1, source_target_pairs={{1,0},{2,1},{3,2},{4,3},{5,4},{6,5},{7,6},{8,7},{9,8},{10,9},{11,1... | collective-permute-start | bytes 393224 | tf_op jit(solution)/shard_map/while/body/eval_jaxpr/ppermute | solution.py:15
  308.4 6.5 %collective-permute-start = (f32[64,512]{1,0:T(8,128)S(1)}, f32[64,512]{1,0:T(8,128)S(1)}, u32[]{:S(2)}, u32[]{:S(2)}) collective-permute-start(f32[64,512]{1,0:T(8,128)S(1)} %convolution_add_fusion.4), channel_id=1, source_target_pairs={{1,0},{2,1},{3,2},{4,3},{5,4},{6,5},{7,6},{8,7},{9,8},{10,9},{11,1... | collective-permute-start | bytes 393224 | tf_op jit(solution)/shard_map/while/body/eval_jaxpr/ppermute | solution.py:15
  319.5 6.5 %collective-permute-start = (f32[64,512]{1,0:T(8,128)S(1)}, f32[64,512]{1,0:T(8,128)S(1)}, u32[]{:S(2)}, u32[]{:S(2)}) collective-permute-start(f32[64,512]{1,0:T(8,128)S(1)} %convolution_add_fusion.4), channel_id=1, source_target_pairs={{1,0},{2,1},{3,2},{4,3},{5,4},{6,5},{7,6},{8,7},{9,8},{10,9},{11,1... | collective-permute-start | bytes 393224 | tf_op jit(solution)/shard_map/while/body/eval_jaxpr/ppermute | solution.py:15
  329.8 6.5 %collective-permute-start = (f32[64,512]{1,0:T(8,128)S(1)}, f32[64,512]{1,0:T(8,128)S(1)}, u32[]{:S(2)}, u32[]{:S(2)}) collective-permute-start(f32[64,512]{1,0:T(8,128)S(1)} %convolution_add_fusion.4), channel_id=1, source_target_pairs={{1,0},{2,1},{3,2},{4,3},{5,4},{6,5},{7,6},{8,7},{9,8},{10,9},{11,1... | collective-permute-start | bytes 393224 | tf_op jit(solution)/shard_map/while/body/eval_jaxpr/ppermute | solution.py:15
  339.6 6.5 %collective-permute-start = (f32[64,512]{1,0:T(8,128)S(1)}, f32[64,512]{1,0:T(8,128)S(1)}, u32[]{:S(2)}, u32[]{:S(2)}) collective-permute-start(f32[64,512]{1,0:T(8,128)S(1)} %convolution_add_fusion.4), channel_id=1, source_target_pairs={{1,0},{2,1},{3,2},{4,3},{5,4},{6,5},{7,6},{8,7},{9,8},{10,9},{11,1... | collective-permute-start | bytes 393224 | tf_op jit(solution)/shard_map/while/body/eval_jaxpr/ppermute | solution.py:15
  359.1 6.5 %collective-permute-start = (f32[64,512]{1,0:T(8,128)S(1)}, f32[64,512]{1,0:T(8,128)S(1)}, u32[]{:S(2)}, u32[]{:S(2)}) collective-permute-start(f32[64,512]{1,0:T(8,128)S(1)} %convolution_add_fusion.4), channel_id=1, source_target_pairs={{1,0},{2,1},{3,2},{4,3},{5,4},{6,5},{7,6},{8,7},{9,8},{10,9},{11,1... | collective-permute-start | bytes 393224 | tf_op jit(solution)/shard_map/while/body/eval_jaxpr/ppermute | solution.py:15
  368.9 6.5 %collective-permute-start = (f32[64,512]{1,0:T(8,128)S(1)}, f32[64,512]{1,0:T(8,128)S(1)}, u32[]{:S(2)}, u32[]{:S(2)}) collective-permute-start(f32[64,512]{1,0:T(8,128)S(1)} %convolution_add_fusion.4), channel_id=1, source_target_pairs={{1,0},{2,1},{3,2},{4,3},{5,4},{6,5},{7,6},{8,7},{9,8},{10,9},{11,1... | collective-permute-start | bytes 393224 | tf_op jit(solution)/shard_map/while/body/eval_jaxpr/ppermute | solution.py:15
  (124 shorter events, 177.1 us)
Async XLA Ops:
  7.2 65.8 %all-gather.3.cloned.1.call-start = ((), (), s32[]{:S(2)}) async-start(), calls=%async_computation | async-start | bytes 8912896 | tf_op jit(solution)/shard_map/all_gather | solution.py:27
  79.2 9.3 %collective-permute-start = (f32[64,512]{1,0:T(8,128)S(1)}, f32[64,512]{1,0:T(8,128)S(1)}, u32[]{:S(2)}, u32[]{:S(2)}) collective-permute-start(f32[64,512]{1,0:T(8,128)S(1)} %convolution_add_fusion.4), channel_id=1, source_target_pairs={{1,0},{2,1},{3,2},{4,3},{5,4},{6,5},{7,6},{8,7},{9,8},{10,9},{11,1... | collective-permute-start | bytes 393224 | tf_op jit(solution)/shard_map/while/body/eval_jaxpr/ppermute | solution.py:15
  89.3 9.0 %collective-permute-start = (f32[64,512]{1,0:T(8,128)S(1)}, f32[64,512]{1,0:T(8,128)S(1)}, u32[]{:S(2)}, u32[]{:S(2)}) collective-permute-start(f32[64,512]{1,0:T(8,128)S(1)} %convolution_add_fusion.4), channel_id=1, source_target_pairs={{1,0},{2,1},{3,2},{4,3},{5,4},{6,5},{7,6},{8,7},{9,8},{10,9},{11,1... | collective-permute-start | bytes 393224 | tf_op jit(solution)/shard_map/while/body/eval_jaxpr/ppermute | solution.py:15
  118.6 9.0 %collective-permute-start = (f32[64,512]{1,0:T(8,128)S(1)}, f32[64,512]{1,0:T(8,128)S(1)}, u32[]{:S(2)}, u32[]{:S(2)}) collective-permute-start(f32[64,512]{1,0:T(8,128)S(1)} %convolution_add_fusion.4), channel_id=1, source_target_pairs={{1,0},{2,1},{3,2},{4,3},{5,4},{6,5},{7,6},{8,7},{9,8},{10,9},{11,1... | collective-permute-start | bytes 393224 | tf_op jit(solution)/shard_map/while/body/eval_jaxpr/ppermute | solution.py:15
  128.3 9.0 %collective-permute-start = (f32[64,512]{1,0:T(8,128)S(1)}, f32[64,512]{1,0:T(8,128)S(1)}, u32[]{:S(2)}, u32[]{:S(2)}) collective-permute-start(f32[64,512]{1,0:T(8,128)S(1)} %convolution_add_fusion.4), channel_id=1, source_target_pairs={{1,0},{2,1},{3,2},{4,3},{5,4},{6,5},{7,6},{8,7},{9,8},{10,9},{11,1... | collective-permute-start | bytes 393224 | tf_op jit(solution)/shard_map/while/body/eval_jaxpr/ppermute | solution.py:15
  138.1 9.1 %collective-permute-start = (f32[64,512]{1,0:T(8,128)S(1)}, f32[64,512]{1,0:T(8,128)S(1)}, u32[]{:S(2)}, u32[]{:S(2)}) collective-permute-start(f32[64,512]{1,0:T(8,128)S(1)} %convolution_add_fusion.4), channel_id=1, source_target_pairs={{1,0},{2,1},{3,2},{4,3},{5,4},{6,5},{7,6},{8,7},{9,8},{10,9},{11,1... | collective-permute-start | bytes 393224 | tf_op jit(solution)/shard_map/while/body/eval_jaxpr/ppermute | solution.py:15
  148.0 10.2 %collective-permute-start = (f32[64,512]{1,0:T(8,128)S(1)}, f32[64,512]{1,0:T(8,128)S(1)}, u32[]{:S(2)}, u32[]{:S(2)}) collective-permute-start(f32[64,512]{1,0:T(8,128)S(1)} %convolution_add_fusion.4), channel_id=1, source_target_pairs={{1,0},{2,1},{3,2},{4,3},{5,4},{6,5},{7,6},{8,7},{9,8},{10,9},{11,1... | collective-permute-start | bytes 393224 | tf_op jit(solution)/shard_map/while/body/eval_jaxpr/ppermute | solution.py:15
  159.0 9.5 %collective-permute-start = (f32[64,512]{1,0:T(8,128)S(1)}, f32[64,512]{1,0:T(8,128)S(1)}, u32[]{:S(2)}, u32[]{:S(2)}) collective-permute-start(f32[64,512]{1,0:T(8,128)S(1)} %convolution_add_fusion.4), channel_id=1, source_target_pairs={{1,0},{2,1},{3,2},{4,3},{5,4},{6,5},{7,6},{8,7},{9,8},{10,9},{11,1... | collective-permute-start | bytes 393224 | tf_op jit(solution)/shard_map/while/body/eval_jaxpr/ppermute | solution.py:15
  169.3 9.0 %collective-permute-start = (f32[64,512]{1,0:T(8,128)S(1)}, f32[64,512]{1,0:T(8,128)S(1)}, u32[]{:S(2)}, u32[]{:S(2)}) collective-permute-start(f32[64,512]{1,0:T(8,128)S(1)} %convolution_add_fusion.4), channel_id=1, source_target_pairs={{1,0},{2,1},{3,2},{4,3},{5,4},{6,5},{7,6},{8,7},{9,8},{10,9},{11,1... | collective-permute-start | bytes 393224 | tf_op jit(solution)/shard_map/while/body/eval_jaxpr/ppermute | solution.py:15
  198.6 9.0 %collective-permute-start = (f32[64,512]{1,0:T(8,128)S(1)}, f32[64,512]{1,0:T(8,128)S(1)}, u32[]{:S(2)}, u32[]{:S(2)}) collective-permute-start(f32[64,512]{1,0:T(8,128)S(1)} %convolution_add_fusion.4), channel_id=1, source_target_pairs={{1,0},{2,1},{3,2},{4,3},{5,4},{6,5},{7,6},{8,7},{9,8},{10,9},{11,1... | collective-permute-start | bytes 393224 | tf_op jit(solution)/shard_map/while/body/eval_jaxpr/ppermute | solution.py:15
  208.4 9.0 %collective-permute-start = (f32[64,512]{1,0:T(8,128)S(1)}, f32[64,512]{1,0:T(8,128)S(1)}, u32[]{:S(2)}, u32[]{:S(2)}) collective-permute-start(f32[64,512]{1,0:T(8,128)S(1)} %convolution_add_fusion.4), channel_id=1, source_target_pairs={{1,0},{2,1},{3,2},{4,3},{5,4},{6,5},{7,6},{8,7},{9,8},{10,9},{11,1... | collective-permute-start | bytes 393224 | tf_op jit(solution)/shard_map/while/body/eval_jaxpr/ppermute | solution.py:15
  218.1 9.2 %collective-permute-start = (f32[64,512]{1,0:T(8,128)S(1)}, f32[64,512]{1,0:T(8,128)S(1)}, u32[]{:S(2)}, u32[]{:S(2)}) collective-permute-start(f32[64,512]{1,0:T(8,128)S(1)} %convolution_add_fusion.4), channel_id=1, source_target_pairs={{1,0},{2,1},{3,2},{4,3},{5,4},{6,5},{7,6},{8,7},{9,8},{10,9},{11,1... | collective-permute-start | bytes 393224 | tf_op jit(solution)/shard_map/while/body/eval_jaxpr/ppermute | solution.py:15
  228.1 10.4 %collective-permute-start = (f32[64,512]{1,0:T(8,128)S(1)}, f32[64,512]{1,0:T(8,128)S(1)}, u32[]{:S(2)}, u32[]{:S(2)}) collective-permute-start(f32[64,512]{1,0:T(8,128)S(1)} %convolution_add_fusion.4), channel_id=1, source_target_pairs={{1,0},{2,1},{3,2},{4,3},{5,4},{6,5},{7,6},{8,7},{9,8},{10,9},{11,1... | collective-permute-start | bytes 393224 | tf_op jit(solution)/shard_map/while/body/eval_jaxpr/ppermute | solution.py:15
  239.3 9.5 %collective-permute-start = (f32[64,512]{1,0:T(8,128)S(1)}, f32[64,512]{1,0:T(8,128)S(1)}, u32[]{:S(2)}, u32[]{:S(2)}) collective-permute-start(f32[64,512]{1,0:T(8,128)S(1)} %convolution_add_fusion.4), channel_id=1, source_target_pairs={{1,0},{2,1},{3,2},{4,3},{5,4},{6,5},{7,6},{8,7},{9,8},{10,9},{11,1... | collective-permute-start | bytes 393224 | tf_op jit(solution)/shard_map/while/body/eval_jaxpr/ppermute | solution.py:15
  249.6 9.0 %collective-permute-start = (f32[64,512]{1,0:T(8,128)S(1)}, f32[64,512]{1,0:T(8,128)S(1)}, u32[]{:S(2)}, u32[]{:S(2)}) collective-permute-start(f32[64,512]{1,0:T(8,128)S(1)} %convolution_add_fusion.4), channel_id=1, source_target_pairs={{1,0},{2,1},{3,2},{4,3},{5,4},{6,5},{7,6},{8,7},{9,8},{10,9},{11,1... | collective-permute-start | bytes 393224 | tf_op jit(solution)/shard_map/while/body/eval_jaxpr/ppermute | solution.py:15
  259.4 9.0 %collective-permute-start = (f32[64,512]{1,0:T(8,128)S(1)}, f32[64,512]{1,0:T(8,128)S(1)}, u32[]{:S(2)}, u32[]{:S(2)}) collective-permute-start(f32[64,512]{1,0:T(8,128)S(1)} %convolution_add_fusion.4), channel_id=1, source_target_pairs={{1,0},{2,1},{3,2},{4,3},{5,4},{6,5},{7,6},{8,7},{9,8},{10,9},{11,1... | collective-permute-start | bytes 393224 | tf_op jit(solution)/shard_map/while/body/eval_jaxpr/ppermute | solution.py:15
  278.9 9.0 %collective-permute-start = (f32[64,512]{1,0:T(8,128)S(1)}, f32[64,512]{1,0:T(8,128)S(1)}, u32[]{:S(2)}, u32[]{:S(2)}) collective-permute-start(f32[64,512]{1,0:T(8,128)S(1)} %convolution_add_fusion.4), channel_id=1, source_target_pairs={{1,0},{2,1},{3,2},{4,3},{5,4},{6,5},{7,6},{8,7},{9,8},{10,9},{11,1... | collective-permute-start | bytes 393224 | tf_op jit(solution)/shard_map/while/body/eval_jaxpr/ppermute | solution.py:15
  288.6 9.0 %collective-permute-start = (f32[64,512]{1,0:T(8,128)S(1)}, f32[64,512]{1,0:T(8,128)S(1)}, u32[]{:S(2)}, u32[]{:S(2)}) collective-permute-start(f32[64,512]{1,0:T(8,128)S(1)} %convolution_add_fusion.4), channel_id=1, source_target_pairs={{1,0},{2,1},{3,2},{4,3},{5,4},{6,5},{7,6},{8,7},{9,8},{10,9},{11,1... | collective-permute-start | bytes 393224 | tf_op jit(solution)/shard_map/while/body/eval_jaxpr/ppermute | solution.py:15
  298.4 9.2 %collective-permute-start = (f32[64,512]{1,0:T(8,128)S(1)}, f32[64,512]{1,0:T(8,128)S(1)}, u32[]{:S(2)}, u32[]{:S(2)}) collective-permute-start(f32[64,512]{1,0:T(8,128)S(1)} %convolution_add_fusion.4), channel_id=1, source_target_pairs={{1,0},{2,1},{3,2},{4,3},{5,4},{6,5},{7,6},{8,7},{9,8},{10,9},{11,1... | collective-permute-start | bytes 393224 | tf_op jit(solution)/shard_map/while/body/eval_jaxpr/ppermute | solution.py:15
  308.4 10.4 %collective-permute-start = (f32[64,512]{1,0:T(8,128)S(1)}, f32[64,512]{1,0:T(8,128)S(1)}, u32[]{:S(2)}, u32[]{:S(2)}) collective-permute-start(f32[64,512]{1,0:T(8,128)S(1)} %convolution_add_fusion.4), channel_id=1, source_target_pairs={{1,0},{2,1},{3,2},{4,3},{5,4},{6,5},{7,6},{8,7},{9,8},{10,9},{11,1... | collective-permute-start | bytes 393224 | tf_op jit(solution)/shard_map/while/body/eval_jaxpr/ppermute | solution.py:15
  319.5 9.5 %collective-permute-start = (f32[64,512]{1,0:T(8,128)S(1)}, f32[64,512]{1,0:T(8,128)S(1)}, u32[]{:S(2)}, u32[]{:S(2)}) collective-permute-start(f32[64,512]{1,0:T(8,128)S(1)} %convolution_add_fusion.4), channel_id=1, source_target_pairs={{1,0},{2,1},{3,2},{4,3},{5,4},{6,5},{7,6},{8,7},{9,8},{10,9},{11,1... | collective-permute-start | bytes 393224 | tf_op jit(solution)/shard_map/while/body/eval_jaxpr/ppermute | solution.py:15
  329.8 9.0 %collective-permute-start = (f32[64,512]{1,0:T(8,128)S(1)}, f32[64,512]{1,0:T(8,128)S(1)}, u32[]{:S(2)}, u32[]{:S(2)}) collective-permute-start(f32[64,512]{1,0:T(8,128)S(1)} %convolution_add_fusion.4), channel_id=1, source_target_pairs={{1,0},{2,1},{3,2},{4,3},{5,4},{6,5},{7,6},{8,7},{9,8},{10,9},{11,1... | collective-permute-start | bytes 393224 | tf_op jit(solution)/shard_map/while/body/eval_jaxpr/ppermute | solution.py:15
  359.1 9.0 %collective-permute-start = (f32[64,512]{1,0:T(8,128)S(1)}, f32[64,512]{1,0:T(8,128)S(1)}, u32[]{:S(2)}, u32[]{:S(2)}) collective-permute-start(f32[64,512]{1,0:T(8,128)S(1)} %convolution_add_fusion.4), channel_id=1, source_target_pairs={{1,0},{2,1},{3,2},{4,3},{5,4},{6,5},{7,6},{8,7},{9,8},{10,9},{11,1... | collective-permute-start | bytes 393224 | tf_op jit(solution)/shard_map/while/body/eval_jaxpr/ppermute | solution.py:15
  368.9 9.0 %collective-permute-start = (f32[64,512]{1,0:T(8,128)S(1)}, f32[64,512]{1,0:T(8,128)S(1)}, u32[]{:S(2)}, u32[]{:S(2)}) collective-permute-start(f32[64,512]{1,0:T(8,128)S(1)} %convolution_add_fusion.4), channel_id=1, source_target_pairs={{1,0},{2,1},{3,2},{4,3},{5,4},{6,5},{7,6},{8,7},{9,8},{10,9},{11,1... | collective-permute-start | bytes 393224 | tf_op jit(solution)/shard_map/while/body/eval_jaxpr/ppermute | solution.py:15
  (13 other events, 734.8 us)
Sparse Core Ops, SparseCore 0:
  10.7 62.2 all-gather.2
